TPU v7x, 32 devices: a whole 2x2x4 slice. The times are simulated.
32 devices in a mesh: frame: 4 (over x, core), cam: 8 (over z, y).
Axes of the slice: x: 2, y: 2, z: 4, core: 2. Of those that a mesh axis runs over, the one named last changes fastest.
Arguments:
- view_maps: bfloat16 [8, 88, 2, 32, 256], P('frame', 'cam'), may hold values from -6 to 6
- conv_weight: bfloat16 [9, 256, 256], replicated, may hold values from -0.125 to 0.125
- join_weight: bfloat16 [16384, 256], P('cam'), may hold values from -0.1875 to 0.1875
- valid_cams: int32 [8, 88], P('frame'), may hold values from 0 to 1, as said below
- latent_grad: bfloat16 [8, 256], P('frame'), may hold values from -6 to 6
Outputs:
- latent: float32 [8, 256], P('frame')
- conv_grad: float32 [9, 256, 256], replicated
- join_grad: float32 [16384, 256], P(('cam', 'frame'))
Inputs may be any that keep to these rules, and one draw needn't show every extreme that they name: `valid_cams`: every frame has at least one usable camera; the last 6 cameras are padding and never usable.
All inputs are finite; a program needn't handle non-finite values.
Results may differ from a plain program's by a relative error of at most 0.007.
Values may be sent and summed in bfloat16 or wider, within the bound.
A program may use at most 64 MiB of HBM per device.

v0:
```python
import jax
import jax.numpy as jnp
from jax import lax
from jax.sharding import PartitionSpec as P


def make_shifts(maps, rows_n, cols_n, chans):
    padded = jnp.pad(maps, ((0, 0), (0, 0), (1, 1), (1, 1), (0, 0)))
    return [
        padded[:, :, dy : dy + rows_n, dx : dx + cols_n, :].reshape(-1, chans)
        for dy in range(3)
        for dx in range(3)
    ]


def on_device(view_maps, conv_weight, join_weight, valid_cams, latent_grad):
    frames_here, cams_here, rows_n, cols_n, chans = view_maps.shape
    feat_len = rows_n * cols_n * chans
    shifted = make_shifts(view_maps, rows_n, cols_n, chans)
    preact = jnp.zeros((frames_here * cams_here * rows_n * cols_n, chans), jnp.float32)
    for k in range(9):
        preact = preact + jnp.dot(shifted[k], conv_weight[k], preferred_element_type=jnp.float32)
    sigma = jax.nn.sigmoid(preact)
    features = (preact * sigma).astype(jnp.bfloat16)
    features = features.reshape(frames_here, cams_here, feat_len)
    slopes = (sigma * (1.0 + preact * (1.0 - sigma))).reshape(frames_here, cams_here, feat_len)
    cam_count = jnp.sum(valid_cams.astype(jnp.float32), axis=1)
    local_valid = lax.dynamic_slice_in_dim(
        valid_cams, lax.axis_index("cam") * cams_here, cams_here, 1
    )
    mask_f = local_valid.astype(jnp.float32)
    mask_b = local_valid.astype(jnp.bfloat16)
    share_len = feat_len // lax.axis_size("cam")
    pooled = lax.psum_scatter(
        jnp.einsum("fc,fcp->pf", mask_b, features, preferred_element_type=jnp.float32),
        "cam",
        scatter_dimension=0,
        tiled=True,
    )
    joined = (pooled.T / cam_count[:, None]).astype(jnp.bfloat16)
    partial_latent = jnp.dot(joined, join_weight, preferred_element_type=jnp.float32)
    latent = lax.psum(partial_latent, "cam")
    joined_grad = jnp.einsum(
        "fl,sl->fs", latent_grad, join_weight, preferred_element_type=jnp.float32
    ).astype(jnp.bfloat16)
    weighting = mask_f / cam_count[:, None]
    scaled = (
        lax.all_gather(joined_grad, "cam", axis=1, tiled=True).astype(jnp.float32)[:, None, :]
        * weighting[:, :, None]
        * slopes
    )
    pre_grad = scaled.astype(jnp.bfloat16)
    pre_grad = pre_grad.reshape(-1, chans)
    taps = jnp.stack(
        [
            lax.dot_general(
                shifted[k], pre_grad, (((0,), (0,)), ((), ())), preferred_element_type=jnp.float32
            )
            for k in range(9)
        ]
    )
    sub_len = share_len // lax.axis_size("frame")
    all_joined, all_cotangent = (
        lax.all_gather(joined, "frame", axis=0, tiled=True),
        lax.all_gather(latent_grad, "frame", axis=0, tiled=True),
    )
    own_rows = lax.dynamic_slice_in_dim(all_joined, lax.axis_index("frame") * sub_len, sub_len, 1)
    join_grad = lax.dot_general(
        own_rows, all_cotangent, (((0,), (0,)), ((), ())), preferred_element_type=jnp.float32
    )
    conv_grad = lax.psum(taps, ("frame", "cam"))
    return (latent, conv_grad, join_grad)


def solution(mesh):
    in_specs = (
        P("frame", "cam", None, None, None),
        P(),
        P("cam", None),
        P("frame", None),
        P("frame", None),
    )
    out_specs = (P("frame", None), P(), P(("cam", "frame"), None))
    return jax.shard_map(
        on_device, mesh=mesh, in_specs=in_specs, out_specs=out_specs, check_vma=False
    )
```

profile of v0, /device:TPU:0, one launch (start us, length us, event | category | flops | bytes accessed | tf_op | source)
XLA Modules:
  0.0 305.6 jit_solution(8454710060224463295)
XLA Ops:
  8.1 4.9 %pad_slice_fusion = (bf16[2,11,2,32,256]{4,3,2,1,0:T(8,128)(2,1)}, bf16[2,11,2,32,256]{4,3,2,1,0:T(8,128)(2,1)}, bf16[2,11,2,32,256]{4,3,2,1,0:T(8,128)(2,1)}, b...) fusion(bf16[2,11,2,32,256]{4,3,2,1,0:T(8,128)(2,1)} %param.5), kind=kLoop, calls=%fused_computation | loop fusion | bytes 6488064 | tf_op jit(solution)/shard_map/slice | solution.py:10
  13.7 32.4 %all_gather.9 = bf16[2,16384]{1,0:T(2,128)(2,1)S(1)} all-gather(bf16[2,2048]{1,0:T(2,128)(2,1)S(1)} %convolution_convert_fusion), channel_id=1, replica_groups=mesh['frame'=4,'cam'=8] {'cam'}, dimensions={1}, use_global_device_ids=true | all-gather | bytes 73728 | tf_op jit(solution)/shard_map/all_gather | solution.py:48
  46.3 1.4 mul.41
  47.7 1.6 fusion.17
  49.8 0.8 copy-done.9
  50.9 0.8 copy-done.7
  52.1 0.8 copy-done.1
  53.2 0.8 copy-done.5
  54.3 0.8 copy-done.3
  55.4 0.8 copy-done.2
  56.5 1.0 copy-done.14
  57.7 1.9 multiply_convert_fusion
  59.6 1.6 reshape.53
  61.6 4.9 %copy.14 = f32[16384,2]{1,0:T(8,128)} copy(f32[16384,2]{0,1:T(2,128)S(1)} %bitcast.140) | data formatting | bytes 262144
  66.6 1.0 copy-done.13
  67.6 2.3 fusion.8
  69.9 1.1 fusion.7
  71.0 1.1 fusion.6
  72.2 1.1 fusion.5
  73.3 1.1 fusion.4
  74.4 1.1 fusion.3
  75.5 1.1 fusion.2
  76.6 1.1 fusion.1
  77.7 1.1 fusion
  78.9 5.1 %all-gather.1 = bf16[4,2,256]{2,1,0:T(2,128)(2,1)S(1)} all-gather(bf16[1,2,256]{2,1,0:T(2,128)(2,1)S(1)} %bitcast.141), channel_id=1, replica_groups=mesh['frame'=4,'cam'=8] {'frame'}, dimensions={0}, use_global_device_ids=true | all-gather | bytes 5120 | tf_op jit(solution)/shard_map/all_gather | solution.py:65
  84.0 142.1 %reduce-scatter.4.cloned.1.call-done = f32[2048,2]{1,0:T(8,128)} async-done(((f32[16384,2]{1,0:T(8,128)}), f32[2048,2]{1,0:T(8,128)}) %reduce-scatter.4.cloned.1.call-update) | async-done | bytes 16400
  226.0 1.6 copy.15
  227.7 5.2 %all-gather = bf16[4,2,2048]{2,1,0:T(2,128)(2,1)S(1)} all-gather(bf16[1,2,2048]{2,1,0:T(2,128)(2,1)S(1)} %fusion.68), channel_id=1, replica_groups=mesh['frame'=4,'cam'=8] {'frame'}, dimensions={0}, use_global_device_ids=true | all-gather | bytes 40960 | tf_op jit(solution)/shard_map/all_gather | solution.py:64
  233.2 20.2 %psum.14 = f32[2,256]{1,0:T(2,128)} all-reduce(f32[2,256]{1,0:T(2,128)S(1)} %fusion.34), channel_id=1, replica_groups=mesh['frame'=4,'cam'=8] {'cam'}, use_global_device_ids=true, to_apply=%region_2.3 | all-reduce | flops 512 | bytes 4096 | tf_op jit(solution)/shard_map/psum | solution.py:42
  253.4 1.1 fusion.28
  254.4 40.5 %all-reduce.3.cloned.1.call-done = f32[9,256,256]{2,1,0:T(8,128)} async-done(((f32[9,256,256]{2,1,0:T(8,128)}), f32[9,256,256]{2,1,0:T(8,128)}) %all-reduce.3.cloned.1.call-update) | async-done | bytes 2359312 | tf_op jit(solution)/shard_map/psum | solution.py:71
  294.9 3.2 %copy.29 = f32[9,256,256]{2,1,0:T(8,128)} copy(f32[9,256,256]{2,1,0:T(8,128)} %all-reduce.3.cloned.1.call-done) | data formatting | bytes 4718592
  (57 shorter events, 4.6 us)
Async XLA Ops:
  8.0 5.3 %copy-start = (bf16[2048,256]{1,0:T(8,128)(2,1)S(1)}, bf16[2048,256]{1,0:T(8,128)(2,1)}, u32[]{:S(2)}) copy-start(bf16[2048,256]{1,0:T(8,128)(2,1)} %param.7) | copy-start | bytes 3145732
  8.0 218.0 %reduce-scatter.4.cloned.1.call-start = ((), (), s32[]{:S(2)}) async-start(), calls=%async_computation.2 | async-start | bytes 9437184
  8.1 5.0 %copy-start.20 = (s32[2,88]{1,0:T(2,128)S(1)}, s32[2,88]{1,0:T(2,128)}, u32[]{:S(2)}) copy-start(s32[2,88]{1,0:T(2,128)} %param.8) | copy-start | bytes 2116
  8.1 5.2 %copy-start.19 = (bf16[2,256]{1,0:T(2,128)(2,1)S(1)}, bf16[2,256]{1,0:T(2,128)(2,1)}, u32[]{:S(2)}) copy-start(bf16[2,256]{1,0:T(2,128)(2,1)} %param.9) | copy-start | bytes 3076
  47.7 1.6 copy-start.11
  47.7 1.7 copy-start.15
  49.5 1.1 copy-start.9
  50.6 1.1 copy-start.7
  51.7 1.1 copy-start.1
  52.8 1.1 copy-start.5
  53.9 1.1 copy-start.3
  55.0 1.1 copy-start.2
  56.1 1.4 copy-start.14
  56.1 1.5 copy-start.16
  66.5 1.1 copy-start.13
  66.5 228.4 %all-reduce.3.cloned.1.call-start = ((), (), s32[]{:S(2)}) async-start(), calls=%async_computation.1 | async-start | bytes 4718592 | tf_op jit(solution)/shard_map/psum | solution.py:71
  66.6 3.3 %copy-start.12 = (bf16[2,11,2,32,256]{4,3,2,1,0:T(8,128)(2,1)S(1)}, bf16[2,11,2,32,256]{4,3,2,1,0:T(8,128)(2,1)}, u32[]{:S(2)}) copy-start(bf16[2,11,2,32,256]{4,3,2,1,0:T(8,128)(2,1)} %get-tuple-element.6) | copy-start | bytes 2162692
  66.6 3.3 %copy-start.18 = (bf16[1408,256]{1,0:T(8,128)(2,1)S(1)}, bf16[1408,256]{1,0:T(8,128)(2,1)}, u32[]{:S(2)}) copy-start(bf16[1408,256]{1,0:T(8,128)(2,1)} %get-tuple-element.3) | copy-start | bytes 2162692
  67.6 3.4 %copy-start.10 = (bf16[2,11,2,32,256]{4,3,2,1,0:T(8,128)(2,1)S(1)}, bf16[2,11,2,32,256]{4,3,2,1,0:T(8,128)(2,1)}, u32[]{:S(2)}) copy-start(bf16[2,11,2,32,256]{4,3,2,1,0:T(8,128)(2,1)} %get-tuple-element.7) | copy-start | bytes 2162692
  69.9 2.2 copy-start.8
  72.2 2.2 copy-start.6
  73.3 2.2 copy-start.4
  75.5 2.2 copy-start.17
Sparse Core Ops, SparseCore 0:
  66.7 159.3 reduce-scatter.3
Sparse Core Ops, SparseCore 1:
  79.0 215.9 all-reduce.2
where the time goes:
time: 306 us
  waiting for transfers between devices  183 us (60%)
  blocking collectives  62.8 us (21%)
  local copies, waits for them, and re-layouts  24.7 us (8%)
  matrix products  19.2 us (6%)
  between operations  15.6 us (5%)
    unnamed x3, waiting for transfers between devices  142 us
    psum x1, waiting for transfers between devices, on_device(): conv_grad = lax.psum(taps, ('frame', 'cam'))  40.5 us
    all_gather x1, blocking collectives, on_device(): lax.all_gather(joined_grad, 'cam', axis=1, tiled=True).astype(jnp.float32)  32.4 us
    psum x1, blocking collectives, on_device(): latent = lax.psum(partial_latent, 'cam')  20.2 us
    unnamed x47, local copies, waits for them, and re-layouts  16.6 us
    dot_general x9, matrix products, on_device(): lax.dot_general(shifted[k], pre_grad, (((0,), (0,)), ((), ())), preferred...  11.2 us
  transfers between devices with their start and end apart: 2, of which 2 were waited for; matrix products, arithmetic and copies ran while one was open for 5% of the time, Pallas kernels for 0%

commit v1 on v0

--- a/solution.py
+++ b/solution.py
@@ -2,6 +2,7 @@
 import jax.numpy as jnp
 from jax import lax
 from jax.sharding import PartitionSpec as P
+from jax.lax import all_to_all, axis_size
 
 
 def make_shifts(maps, rows_n, cols_n, chans):
@@ -45,7 +46,15 @@
     ).astype(jnp.bfloat16)
     weighting = mask_f / cam_count[:, None]
     scaled = (
-        lax.all_gather(joined_grad, "cam", axis=1, tiled=True).astype(jnp.float32)[:, None, :]
+        jnp.concatenate(
+            all_to_all(
+                jnp.stack([joined_grad for _ in range(axis_size("cam"))], axis=0),
+                split_axis=0,
+                axis_name="cam",
+                concat_axis=0,
+            ),
+            axis=1,
+        ).astype(jnp.float32)[:, None, :]
         * weighting[:, :, None]
         * slopes
     )

time: 306 us -> 287 us (0.938)
  blocking collectives: 62.8 us -> 30.4 us
  waiting for transfers between devices: 183 us -> 193 us
  starting transfers between devices: 0.08 us -> 7.39 us
  matrix products: 19.2 us -> 15.6 us
    all_gather x1 -> x0, blocking collectives: 32.4 us -> none  [on_device(): lax.all_gather(joined_grad, 'cam', axis=1, tiled=True).astype(jnp.float32)]
    unnamed x3, waiting for transfers between devices: 142 us -> 152 us
    all_to_all x0 -> x1, starting transfers between devices: none -> 7.31 us  [on_device(): all_to_all(jnp.stack([joined_grad for _ in range(axis_size('cam'))], axis...]
    dot_general x9, matrix products: 11.2 us -> 4.42 us  [on_device(): lax.dot_general(shifted[k], pre_grad, (((0,), (0,)), ((), ())), preferred...]
  transfers between devices with their start and end apart: 2 -> 3, of which waited for: 2 -> 2; matrix products, arithmetic and copies ran while one was open for 5% -> 4% of each run, Pallas kernels for 0% -> 0%
where the time goes in v1:
time: 287 us; the launch traced here: 286 us
  waiting for transfers between devices  193 us (67%)
  blocking collectives  30.4 us (11%)
  local copies, waits for them, and re-layouts  23.5 us (8%)
  between operations  15.8 us (6%)
  matrix products  15.6 us (5%)
  starting transfers between devices  7.39 us (3%)
    unnamed x3, waiting for transfers between devices  152 us
    psum x1, waiting for transfers between devices, on_device(): conv_grad = lax.psum(taps, ('frame', 'cam'))  40.5 us
    psum x1, blocking collectives, on_device(): latent = lax.psum(partial_latent, 'cam')  20.2 us
    unnamed x47, local copies, waits for them, and re-layouts  18 us
    dot_general x9, matrix products, on_device(): jnp.dot(shifted[k], conv_weight[k], preferred_element_type=jnp.float32)  8.53 us
    all_to_all x1, starting transfers between devices, on_device(): all_to_all(jnp.stack([joined_grad for _ in range(axis_size('cam'))], axis...  7.31 us
  transfers between devices with their start and end apart: 3, of which 2 were waited for; matrix products, arithmetic and copies ran while one was open for 4% of the time, Pallas kernels for 0%

profile of v1, /device:TPU:0, one launch (start us, length us, event | category | flops | bytes accessed | tf_op | source)
XLA Modules:
  0.0 285.9 jit_solution(14921966231475837991)
XLA Ops:
  8.0 1.2 copy-done
  9.2 1.0 convolution_convert_fusion
  10.3 0.7 stack.41
  11.0 7.3 %all-to-all-start = ((bf16[8,2,2048]{2,1,0:T(2,128)(2,1)}), bf16[8,2,2048]{2,1,0:T(2,128)(2,1)S(1)}, u32[]{:S(2)}, u32[]{:S(2)}) async-start(bf16[8,2,2048]{2,1,0:T(2,128)(2,1)} %stack.41), calls=%async_computation | async-start | bytes 131072 | tf_op jit(solution)/shard_map/all_to_all | solution.py:50
  18.3 2.8 pad_slice_fusion
  21.3 2.1 fusion.17
  23.8 0.8 copy-done.11
  24.9 0.8 copy-done.9
  26.4 0.8 copy-done.7
  27.8 1.5 convolution_add_fusion.1
  29.7 1.4 mul.41
  31.1 3.0 %multiply_convert_fusion = (bf16[1408,256]{1,0:T(8,128)(2,1)S(1)}, bf16[1408,256]{1,0:T(8,128)(2,1)S(1)}) fusion(f32[1408,256]{1,0:T(8,128)} %mul.41, f32[1408,256]{1,0:T(8,128)} %convolution_add_fusion.1, bf16[1408,256]{1,0:T(8,128)(2,1)} %bitcast.141, bf16[9,256,256]{2,1,0:T(8,128)(2,1)} %param.6), kind=kOutput, calls=%fused_computation.17 | convolution fusion | flops 188874752 | bytes 5177344 | tf_op jit(solution)/shard_map/dot_general | solution.py:23
  34.5 0.7 copy-done.14
  35.2 0.4 fusion.7
  35.7 0.4 fusion.6
  36.4 0.4 fusion.5
  36.8 0.4 fusion.4
  38.7 0.4 fusion.1
  39.1 1.4 copy-done.16
  40.5 0.5 reshape.63
  41.4 5.0 %copy.14 = f32[16384,2]{1,0:T(8,128)} copy(f32[16384,2]{0,1:T(2,128)S(1)} %bitcast.143) | data formatting | bytes 262144
  46.4 1.0 copy-done.18
  47.5 1.1 fusion
  48.6 0.6 copy-done.19
  49.3 5.1 %all-gather.1 = bf16[4,2,256]{2,1,0:T(2,128)(2,1)S(1)} all-gather(bf16[1,2,256]{2,1,0:T(2,128)(2,1)S(1)} %bitcast.145), channel_id=1, replica_groups=mesh['frame'=4,'cam'=8] {'frame'}, dimensions={0}, use_global_device_ids=true | all-gather | bytes 5120 | tf_op jit(solution)/shard_map/all_gather | solution.py:74
  54.3 152.0 %reduce-scatter.4.cloned.1.call-done = f32[2048,2]{1,0:T(8,128)} async-done(((f32[16384,2]{1,0:T(8,128)}), f32[2048,2]{1,0:T(8,128)}) %reduce-scatter.4.cloned.1.call-update) | async-done | bytes 16400
  206.3 1.6 copy.15
  208.0 5.2 %all-gather = bf16[4,2,2048]{2,1,0:T(2,128)(2,1)S(1)} all-gather(bf16[1,2,2048]{2,1,0:T(2,128)(2,1)S(1)} %fusion.68), channel_id=1, replica_groups=mesh['frame'=4,'cam'=8] {'frame'}, dimensions={0}, use_global_device_ids=true | all-gather | bytes 40960 | tf_op jit(solution)/shard_map/all_gather | solution.py:73
  213.5 20.2 %psum.14 = f32[2,256]{1,0:T(2,128)} all-reduce(f32[2,256]{1,0:T(2,128)S(1)} %fusion.34), channel_id=1, replica_groups=mesh['frame'=4,'cam'=8] {'cam'}, use_global_device_ids=true, to_apply=%region_2.3 | all-reduce | flops 512 | bytes 4096 | tf_op jit(solution)/shard_map/psum | solution.py:43
  233.7 1.1 fusion.28
  234.7 40.5 %all-reduce.3.cloned.1.call-done = f32[9,256,256]{2,1,0:T(8,128)} async-done(((f32[9,256,256]{2,1,0:T(8,128)}), f32[9,256,256]{2,1,0:T(8,128)}) %all-reduce.3.cloned.1.call-update) | async-done | bytes 2359312 | tf_op jit(solution)/shard_map/psum | solution.py:80
  275.2 3.2 %copy.29 = f32[9,256,256]{2,1,0:T(8,128)} copy(f32[9,256,256]{2,1,0:T(8,128)} %all-reduce.3.cloned.1.call-done) | data formatting | bytes 4718592
  (59 shorter events, 5.8 us)
Async XLA Ops:
  8.0 1.2 copy-start
  8.0 10.3 %copy-start.1 = (bf16[2,11,2,32,256]{4,3,2,1,0:T(8,128)(2,1)S(1)}, bf16[2,11,2,32,256]{4,3,2,1,0:T(8,128)(2,1)}, u32[]{:S(2)}) copy-start(bf16[2,11,2,32,256]{4,3,2,1,0:T(8,128)(2,1)} %param.5) | copy-start | bytes 2162692
  11.0 18.5 %all-to-all-start = ((bf16[8,2,2048]{2,1,0:T(2,128)(2,1)}), bf16[8,2,2048]{2,1,0:T(2,128)(2,1)S(1)}, u32[]{:S(2)}, u32[]{:S(2)}) async-start(bf16[8,2,2048]{2,1,0:T(2,128)(2,1)} %stack.41), calls=%async_computation | async-start | bytes 131072 | tf_op jit(solution)/shard_map/all_to_all | solution.py:50
  18.3 188.1 %reduce-scatter.4.cloned.1.call-start = ((), (), s32[]{:S(2)}) async-start(), calls=%async_computation.3 | async-start | bytes 9437184
  18.3 2.8 copy-start.20
  21.1 6.3 %copy-start.5 = (bf16[2,11,2,32,256]{4,3,2,1,0:T(8,128)(2,1)}, bf16[2,11,2,32,256]{4,3,2,1,0:T(8,128)(2,1)S(1)}, u32[]{:S(2)}) copy-start(bf16[2,11,2,32,256]{4,3,2,1,0:T(8,128)(2,1)S(1)} %get-tuple-element.10) | copy-start | bytes 2162692
  21.1 6.7 %copy-start.3 = (bf16[2,11,2,32,256]{4,3,2,1,0:T(8,128)(2,1)}, bf16[2,11,2,32,256]{4,3,2,1,0:T(8,128)(2,1)S(1)}, u32[]{:S(2)}) copy-start(bf16[2,11,2,32,256]{4,3,2,1,0:T(8,128)(2,1)S(1)} %get-tuple-element.11) | copy-start | bytes 2162692
  21.2 2.2 copy-start.13
  21.2 2.3 copy-start.17
  23.4 1.1 copy-start.11
  24.5 1.1 copy-start.9
  26.0 1.1 copy-start.7
  31.1 3.0 %copy-start.15 = (bf16[2,11,2,32,256]{4,3,2,1,0:T(8,128)(2,1)S(1)}, bf16[2,11,2,32,256]{4,3,2,1,0:T(8,128)(2,1)}, u32[]{:S(2)}) copy-start(bf16[2,11,2,32,256]{4,3,2,1,0:T(8,128)(2,1)} %get-tuple-element.12) | copy-start | bytes 2162692
  34.1 1.1 copy-start.14
  34.1 1.5 copy-start.12
  35.2 1.2 copy-start.10
  35.6 1.2 copy-start.2
  36.4 1.2 copy-start.8
  36.8 1.2 copy-start.6
  37.5 1.2 copy-start.4
  39.1 1.4 copy-start.16
  46.4 1.1 copy-start.18
  46.4 228.8 %all-reduce.3.cloned.1.call-start = ((), (), s32[]{:S(2)}) async-start(), calls=%async_computation.2 | async-start | bytes 4718592 | tf_op jit(solution)/shard_map/psum | solution.py:80
  48.6 0.7 copy-start.19
Sparse Core Ops, SparseCore 0:
  46.5 159.7 reduce-scatter.3
Sparse Core Ops, SparseCore 1:
  53.0 222.2 all-reduce.2
